TPU v7x, 32 devices: a whole 2x2x4 slice. The times are simulated.
32 devices in a mesh: atom: 16 (over z, x, core), energy: 2 (over y).
Axes of the slice: x: 2, y: 2, z: 4, core: 2. Of those that a mesh axis runs over, the one named last changes fastest.
Arguments:
- single_site: float32 [256, 2, 2, 1024], P('atom', 'energy'), may hold values from -2 to 2
- structure: float32 [2, 26, 2, 1024], P('energy'), may hold values from -0.4375 to 0.4375
- neighbours: int32 [256, 26], P('atom'), may hold values from 0 to 255, as said below
- species: int32 [256], P('atom'), may hold values from 0 to 1
- valence: float32 [2], replicated, may hold values from 0.5 to 3
- energy_weights: float32 [2, 2], P('energy'), may hold values from -4 to 4
- gaunt_table: float32 [49, 1024], replicated, may hold values from -1.5 to 1.5
- radial_shapes: float32 [2, 2, 2, 49, 512], P(None, 'energy'), may hold values from -6 to 6
- radial_weights: float32 [512], replicated, may hold values from 0.001 to 0.03
- madelung: float32 [256, 256], P('atom'), may hold values from -0.375 to 0.375
- old_potential: float32 [256, 49, 512], P('atom', None, 'energy'), may hold values from -6 to 6
Outputs:
- density: float32 [256, 49, 512], P('atom', None, 'energy')
- potential: float32 [256, 49, 512], P('atom', None, 'energy')
Inputs may be any that keep to these rules, and one draw needn't show every extreme that they name: `neighbours`: atom a lies in lattice plane a // 16; the 16 planes close periodically. Slots 0 to 8 name distinct atoms of the plane before a's, slots 9 to 16 distinct atoms of a's own plane other than a, slots 17 to 25 distinct atoms of the plane after. Direction 26 - 1 - k is the reverse of direction k; this only says which structure constants pair up, and the neighbour lists need not be reciprocal.
All inputs are finite; a program needn't handle non-finite values.
Results may differ from a plain program's by a relative error of at most 0.0001.
Values sent between devices are 32-bit elements; how exact they have to be, the bound alone decides.
A program may use at most 64 MiB of HBM per device.

v0:
```python
import functools

import jax
import jax.numpy as jnp
from jax import lax
from jax.experimental import pallas as pl
from jax.experimental.pallas import tpu as pltpu
from jax.sharding import PartitionSpec as P

PLANE = 16
TERMS = 4
LANES = 128

mixing = 0.3
f32 = jnp.float32
bf16 = jnp.bfloat16


def split(x):
    high = x.astype(bf16)
    return high, (x - high.astype(f32)).astype(bf16)


def tile_masks(rows):
    lane = lax.broadcasted_iota(jnp.int32, (rows, LANES), 1)
    return lane < 64, (lane & 32) == 0


def times_i(x, real_lane):
    return jnp.where(real_lane, -pltpu.roll(x, 96, 1), pltpu.roll(x, 32, 1))


def dot(a, b):
    return jnp.dot(a, b, preferred_element_type=f32)


def to_rows(raw, tiles, w_ref, order):
    stride = w_ref.shape[0] // order
    lane = lax.broadcasted_iota(jnp.int32, (tiles, LANES), 1) // 32
    for block in range(order // 4):
        parts = [raw(m, pl.ds(block * LANES, LANES)) for m in range(4)]
        for ii in range(4):
            u = None
            for m in range(4):
                shift = ((m - ii) * 32) % LANES
                x = parts[m] if shift == 0 else pltpu.roll(parts[m], shift, 1)
                u = x if u is None else jnp.where(lane == m, x, u)
            w_ref[pl.ds((4 * block + ii) * stride, tiles), :] = u


def tile_of(w_ref, tile, order):
    return w_ref[pl.ds(tile, order, stride=w_ref.shape[0] // order), :]


def prepare_couplings(w_ref, rhs_ref, g2_ref, order, blocks):
    _, real_lane = tile_masks(order)
    lane = lax.broadcasted_iota(jnp.int32, (order, LANES), 1) // 32
    joined = [None] * 4
    for t in range(blocks):
        g = tile_of(w_ref, t, order)
        high, low = split(jnp.concatenate([g, times_i(g, real_lane)], axis=0))
        rhs_ref[:, pl.ds(t * LANES, LANES)] = jnp.concatenate([high, high, low, low], axis=0)
    for t in range(blocks):
        g = tile_of(w_ref, blocks - 1 - t, order)
        place = t % 4
        for parity in range(2):
            for z in range(2):
                row = parity * 2 + z
                chunk = (2 - 2 * parity + z) % 4
                shift = ((place - chunk) * 32) % LANES
                x = g if shift == 0 else pltpu.roll(g, shift, 1)
                joined[row] = x if place == 0 else jnp.where(lane == place, x, joined[row])
                if place == 3 or t == blocks - 1:
                    lanes = pl.ds(t // 4 * LANES, 32 * (place + 1))
                    high, low = split(joined[row][:, : 32 * (place + 1)])
                    g2_ref[pl.ds(row * order, order), lanes] = high
                    g2_ref[pl.ds((4 + row) * order, order), lanes] = low


def plane_products(x, lhs_ref, rhs_ref, rhigh_ref, rlow_ref, plane, first, count, order):
    low_lane, _ = tile_masks(order)
    for pair in range(PLANE // 2):
        v = x(pair)
        high = v.astype(bf16).astype(f32)
        low = v - high
        even = jnp.where(low_lane, high, pltpu.roll(low, 64, 1))
        odd = jnp.where(low_lane, pltpu.roll(high, 64, 1), low)
        lhs_ref[pl.ds(pair * 2 * order, 2 * order), :] = jnp.concatenate(
            [even, odd], axis=0
        ).astype(bf16)
    lhs = lhs_ref[...]
    lhs = jnp.concatenate([lhs, lhs], axis=1)
    for t in range(count):
        r = dot(lhs, rhs_ref[:, pl.ds((first + t) * LANES, LANES)])
        high, low = split(r)
        rhigh_ref[plane, t] = high.reshape(PLANE, order, LANES)
        rlow_ref[plane, t] = low.reshape(PLANE, order, LANES)


def gather(nbr_ref, rhigh_ref, rlow_ref, yhigh_ref, ylow_ref, dirs, plane, first, order):
    start, stop = ends_of(dirs)[plane]
    for k in range(start, stop):
        b = dirs - 1 - k
        t = b // 2
        half = slice((b % 2) * 64, (b % 2) * 64 + 64)
        for a in range(PLANE):
            n = nbr_ref[a, k] & (PLANE - 1)
            to = (pl.ds(t * order, order), pl.ds(a * LANES + (b % 2) * 64, 64))
            yhigh_ref[to] = rhigh_ref[plane, t - first, n][:, half]
            ylow_ref[to] = rlow_ref[plane, t - first, n][:, half]


def block_diagonal(v, low_lane, real_lane):
    turned = times_i(v, real_lane)
    zero = jnp.zeros_like(v)
    return jnp.concatenate(
        [
            jnp.where(low_lane, v, zero),
            jnp.where(low_lane, turned, zero),
            jnp.where(low_lane, zero, v),
            jnp.where(low_lane, zero, turned),
        ],
        axis=0,
    )


def weights_of(v, low_lane, real_lane):
    high, low = split(block_diagonal(v, low_lane, real_lane))
    return jnp.concatenate([high, low], axis=1)


def pair_product(u, weights, order):
    high, low = split(u)
    o = dot(jnp.concatenate([high, low], axis=0), weights)
    return o[:order, :LANES] + o[order:, :LANES] + o[:order, LANES:]


def path_and_project(own, g2_ref, yhigh_ref, ylow_ref, wt_ref, gaunt_ref, v_ref, order):
    low_lane, real_lane = tile_masks(order)
    low2, _ = tile_masks(2 * order)
    both = g2_ref[...]
    rows = both.shape[0] // 2
    half = rows // 2
    gh = both[:rows]
    pairs = range(PLANE // 2)
    cs = []
    for pair in pairs:
        lanes = pl.ds(pair * 2 * LANES, 2 * LANES)
        d = dot(both, yhigh_ref[:, lanes])
        s = d[:rows] + d[rows:] + dot(gh, ylow_ref[:, lanes])
        e0, o0 = s[:half, :LANES], s[half:, :LANES]
        e1, o1 = s[:half, LANES:], s[half:, LANES:]
        m = jnp.where(low2, e0, o1) + pltpu.roll(jnp.where(low2, e1, o0), 64, 1)
        cs.append(m[:order] + times_i(m[order:], real_lane))
    qs = [pair_product(cs[pair], wt_ref[pair], order) for pair in pairs]
    ws = [weights_of(q, low_lane, real_lane) for q in qs]
    ts = [own(pair) for pair in pairs]
    vs = ts
    for _ in range(TERMS - 1):
        vs = [ts[pair] + pair_product(vs[pair], ws[pair], order) for pair in pairs]
    for pair in pairs:
        v_ref[pl.ds(pair * order, order), :] = vs[pair]
    pairs = PLANE // 2
    lane = lax.broadcasted_iota(jnp.int32, (pairs, LANES), 1) // 32
    columns = []
    for block in range(order // 4):
        us = [v_ref[pl.ds(4 * block + ii, pairs, stride=order), :] for ii in range(4)]
        pieces = []
        for part in range(4):
            z = us[0] if part == 0 else pltpu.roll(us[0], (-part * 32) % LANES, 1)
            for ii in range(1, 4):
                shift = ((ii - part) * 32) % LANES
                z = jnp.where(lane == ii, us[ii] if shift == 0 else pltpu.roll(us[ii], shift, 1), z)
            pieces.append(z)
        columns.append(jnp.concatenate(pieces, axis=0))
    z = jnp.concatenate(columns, axis=1)
    zh, zl = split(z)
    gh, gl = gaunt_ref[0], gaunt_ref[1]
    nt = (((1,), (1,)), ((), ()))
    d = lax.dot_general(jnp.concatenate([zh, zl], axis=0), gh, nt, preferred_element_type=f32)
    return d[: 2 * PLANE] + d[2 * PLANE :] + lax.dot_general(zh, gl, nt, preferred_element_type=f32)


def store_scaled(projected, wr, wi, coef_ref):
    pairs = PLANE // 2
    for a2 in range(2):
        re = projected[a2 * 2 * pairs : a2 * 2 * pairs + pairs]
        im = projected[a2 * 2 * pairs + pairs : (a2 + 1) * 2 * pairs]
        coef_ref[0, pl.ds(a2, pairs, stride=2), :] = wr * re - wi * im
        coef_ref[1, pl.ds(a2, pairs, stride=2), :] = wr * im + wi * re


def ends_of(dirs):
    return ((0, 9), (9, 17), (17, dirs))


def plan(dirs):
    ends = ends_of(dirs)
    firsts = tuple((dirs - stop) // 2 for _, stop in ends)
    counts = tuple((dirs - 1 - start) // 2 - first + 1 for (start, _), first in zip(ends, firsts))
    return firsts, counts


def density_of(kind, coef_ref, pieces_ref, old_ref, density_ref, mixed_ref):
    energies, kinds = pieces_ref.shape[:2]
    channels, atoms, width = density_ref.shape
    kind = jnp.broadcast_to(kind, (atoms, width))
    for l in range(channels):
        total = None
        for e in range(energies):
            for z in range(2):
                row = jnp.broadcast_to(pieces_ref[e, 0, l, 1 - z : 2 - z, :], (atoms, width))
                for s in range(1, kinds):
                    row = jnp.where(kind == s, pieces_ref[e, s, l, 1 - z : 2 - z, :], row)
                term = coef_ref[e, z, :, l : l + 1] * row
                total = term if total is None else total + term
        density_ref[l] = total
        if l > 0:
            mixed_ref[l - 1] = (1.0 - mixing) * old_ref[l] + mixing * total


def core(order, dirs, ring, energies, nbr_ref, w_ref, valence_ref, own_ref, g_ref, gaunt_ref, shapes_ref,
         weights_ref, species_ref, madelung_ref, previous_ref, density_ref, potential_ref,
         coef_ref, pieces_ref, total_ref, old_ref, mixed_ref, first_ref, wd_ref, table_ref, halo_ref, q_ref, mine_ref, wg_ref, wt_ref, rhs_ref, g2_ref, lhs_ref, rhigh_ref, rlow_ref,
         yhigh_ref, ylow_ref, v_ref, halo_send, halo_recv, piece_send, piece_recv, coef_send, coef_recv,
         q_send, q_recv, local_sem, old_sem, mixed_sem, first_sem):
    atom, energy = lax.axis_index("atom"), lax.axis_index("energy")
    devices = ring * energies
    me = atom * energies + energy
    kinds, width = shapes_ref.shape[0], pieces_ref.shape[4]

    def place(step):
        other = lax.rem(me + step, devices)
        return {"atom": other // energies, "energy": lax.rem(other, energies)}

    fetch = pltpu.make_async_copy(previous_ref, old_ref, old_sem)
    fetch.start()
    barrier = pltpu.get_barrier_semaphore()

    def greet(step, carry):
        pl.semaphore_signal(barrier, inc=1, device_id=place(step), device_id_type=MESH)
        return carry

    lax.fori_loop(1, devices, greet, 0)

    firsts, counts = plan(dirs)
    to_rows(lambda m, lanes: g_ref[:, m // 2, m % 2, lanes], dirs // 2, wg_ref, order)
    prepare_couplings(wg_ref, rhs_ref, g2_ref, order, dirs // 2)
    pl.semaphore_wait(barrier, devices - 1)

    right, left = lax.rem(atom + 1, ring), lax.rem(atom + ring - 1, ring)
    halos = []
    for side, target in ((0, right), (1, left)):
        copy = pltpu.make_async_remote_copy(
            src_ref=own_ref, dst_ref=halo_ref.at[side], send_sem=halo_send.at[side],
            recv_sem=halo_recv.at[side], device_id={"atom": target, "energy": energy}, device_id_type=MESH,
        )
        copy.start()
        halos.append(copy)

    def slice_of(e):
        return shapes_ref.at[:, :, :, pl.ds(pl.multiple_of(e * width, LANES), width)]

    pieces = []
    for step in range(1, energies):
        other = lax.rem(energy + step, energies)
        copy = pltpu.make_async_remote_copy(
            src_ref=slice_of(other), dst_ref=pieces_ref.at[energy], send_sem=piece_send.at[step],
            recv_sem=piece_recv.at[step], device_id={"atom": atom, "energy": other}, device_id_type=MESH,
        )
        copy.start()
        pieces.append(copy)
    keep = pltpu.make_async_copy(slice_of(energy), pieces_ref.at[energy], local_sem)
    keep.start()

    def plane(index, raw):
        w = wt_ref.at[index]
        to_rows(raw, PLANE // 2, w, order)
        plane_products(lambda pair: tile_of(w, pair, order), lhs_ref, rhs_ref, rhigh_ref, rlow_ref,
                       index, firsts[index], counts[index], order)
        gather(nbr_ref, rhigh_ref, rlow_ref, yhigh_ref, ylow_ref, dirs, index, firsts[index], order)

    plane(1, lambda m, lanes: own_ref[:, m // 2, m % 2, lanes])

    low_lane, real_lane = tile_masks(order)
    for pair in range(PLANE // 2):
        wd_ref[pair] = weights_of(tile_of(wt_ref.at[1], pair, order), low_lane, real_lane)
    table_ref[0], table_ref[1] = split(gaunt_ref[...])

    row = lax.broadcasted_iota(jnp.int32, (PLANE, PLANE), 0)
    lane = lax.broadcasted_iota(jnp.int32, (PLANE, PLANE), 1)
    kinds_row = jnp.broadcast_to(species_ref[...].astype(f32), (PLANE, PLANE))
    kind = jnp.sum(jnp.where(row == lane, kinds_row, jnp.zeros((PLANE, PLANE), f32)), axis=1, keepdims=True)
    sums = [None, None]
    base = jnp.zeros(kind.shape, f32)
    for s in range(kinds):
        total = jnp.sum(shapes_ref[s, 0] * weights_ref[...], axis=1, keepdims=True)
        for z in range(2):
            value = jnp.broadcast_to(total[1 - z : 2 - z], kind.shape)
            sums[z] = value if s == 0 else jnp.where(kind == s, value, sums[z])
        base = jnp.where(kind == s, valence_ref[s], base)
    base = jnp.where(energy == 0, base, jnp.zeros_like(base))

    for side, index in ((0, 0), (1, 2)):
        halos[side].wait_recv()
        plane(index, lambda m, lanes, side=side: halo_ref[side, :, m // 2, m % 2, lanes])

    own = lambda pair: tile_of(wt_ref.at[1], pair, order)
    projected = path_and_project(own, g2_ref, yhigh_ref, ylow_ref, wd_ref, table_ref, v_ref, order)
    store_scaled(projected, w_ref[0, 0], w_ref[0, 1], mine_ref)

    q = mine_ref[0, :, 0:1] * sums[0] + mine_ref[1, :, 0:1] * sums[1] - base
    row = lax.broadcasted_iota(jnp.int32, (PLANE, LANES), 0)
    lane = lax.broadcasted_iota(jnp.int32, (PLANE, LANES), 1)
    spot = lane == row + PLANE * lax.rem(atom, LANES // PLANE)
    q_ref[me] = jnp.sum(jnp.where(spot, q, jnp.zeros((PLANE, LANES), f32)), axis=0, keepdims=True)

    def spread(step, carry):
        pltpu.make_async_remote_copy(
            src_ref=q_ref.at[me], dst_ref=q_ref.at[me], send_sem=q_send, recv_sem=q_recv,
            device_id=place(step), device_id_type=MESH,
        ).start()
        return carry

    lax.fori_loop(1, devices, spread, 0)
    coefs = []
    for step in range(1, energies):
        other = lax.rem(energy + step, energies)
        copy = pltpu.make_async_remote_copy(
            src_ref=mine_ref, dst_ref=coef_ref.at[energy], send_sem=coef_send.at[step],
            recv_sem=coef_recv.at[step], device_id={"atom": atom, "energy": other}, device_id_type=MESH,
        )
        copy.start()
        coefs.append(copy)
    coef_ref[energy] = mine_ref[...]

    keep.wait()
    for copy in pieces + coefs:
        copy.wait()
    fetch.wait()
    density_of(kind, coef_ref, pieces_ref, old_ref, total_ref, mixed_ref)
    out = pltpu.make_async_copy(total_ref, density_ref, local_sem)
    out.start()
    upper = pltpu.make_async_copy(mixed_ref, potential_ref.at[pl.ds(1, mixed_ref.shape[0])], mixed_sem)
    upper.start()
    for copy in halos:
        copy.wait_send()
    rest = q_ref.at[pl.ds(0, devices - 1)]
    pltpu.make_async_copy(rest, rest, q_send).wait()
    pltpu.make_async_copy(rest, rest, q_recv).wait()
    group = LANES // PLANE * energies
    shift = jnp.zeros((PLANE, 1), f32)
    for g in range(ring * PLANE // LANES):
        charges = jnp.sum(q_ref[pl.ds(g * group, group), 0, :], axis=0, keepdims=True)
        shift = shift + jnp.sum(madelung_ref[:, pl.ds(g * LANES, LANES)] * charges, axis=1, keepdims=True)
    first_ref[0] = (1.0 - mixing) * old_ref[0] + mixing * (total_ref[0] + shift)
    last = pltpu.make_async_copy(first_ref, potential_ref.at[pl.ds(0, 1)], first_sem)
    last.start()
    out.wait()
    upper.wait()
    last.wait()


def core_scratch(order, dirs, ring, energies, channels, kinds, width):
    count = max(plan(dirs)[1])
    depth = dirs // 2 * order
    dma = pltpu.SemaphoreType.DMA
    return [
        pltpu.VMEM((energies, 2, PLANE, channels), f32),
        pltpu.VMEM((energies, kinds, channels, 2, width), f32),
        pltpu.VMEM((channels, PLANE, width), f32),
        pltpu.VMEM((channels, PLANE, width), f32),
        pltpu.VMEM((channels - 1, PLANE, width), f32),
        pltpu.VMEM((1, PLANE, width), f32),
        pltpu.VMEM((PLANE // 2, LANES, 2 * LANES), bf16),
        pltpu.VMEM((2, channels, order * order), bf16),
        pltpu.VMEM((2, PLANE // 2, 2, 2, order * order), f32),
        pltpu.VMEM((ring * energies, 1, LANES), f32),
        pltpu.VMEM((2, PLANE, channels), f32),
        pltpu.VMEM((order * 16, LANES), f32),
        pltpu.VMEM((3, order * (PLANE // 2), LANES), f32),
        pltpu.VMEM((8 * order, dirs * 64), bf16),
        pltpu.VMEM((8 * order, depth), bf16),
        pltpu.VMEM((PLANE * order, LANES), bf16),
        pltpu.VMEM((3, count, PLANE, order, LANES), bf16),
        pltpu.VMEM((3, count, PLANE, order, LANES), bf16),
        pltpu.VMEM((depth, PLANE * LANES), bf16),
        pltpu.VMEM((depth, PLANE * LANES), bf16),
        pltpu.VMEM((PLANE // 2 * order, LANES), f32),
        dma((2,)), dma((2,)), dma((energies,)), dma((energies,)), dma((energies,)), dma((energies,)),
        dma, dma, dma, dma, dma, dma,
    ]


VMEM = pl.BlockSpec(memory_space=pltpu.VMEM)
SMEM = pl.BlockSpec(memory_space=pltpu.SMEM)
ANY = pl.BlockSpec(memory_space=pl.ANY)
MESH = pl.DeviceIdType.MESH


def shards(single_site, structure, neighbours, species, valence, energy_weights, gaunt_table,
           radial_shapes, radial_weights, madelung, old_potential):
    atom_rows, energy_rows = single_site.shape[:2]
    dirs = structure.shape[1]
    order = int(round(single_site.shape[3] ** 0.5))
    channels, width = old_potential.shape[1], old_potential.shape[2]
    kinds = radial_shapes.shape[0]
    energies = lax.axis_size("energy")
    assert atom_rows == PLANE and energy_rows == 1 and order == 32

    def parts(x):
        return x.reshape(-1, 2, 2, order * order)

    shapes = jnp.transpose(radial_shapes[:, 0], (0, 2, 1, 3))
    ring = lax.axis_size("atom")
    density, potential = pl.pallas_call(
        functools.partial(core, order, dirs, ring, energies),
        out_shape=[jax.ShapeDtypeStruct((channels, atom_rows, width), f32)] * 2,
        in_specs=[SMEM] * 3 + [VMEM] * 7 + [ANY],
        out_specs=[ANY] * 2,
        scratch_shapes=core_scratch(order, dirs, ring, energies, channels, kinds, width),
        compiler_params=pltpu.CompilerParams(collective_id=0, has_side_effects=True),
        name="scatter",
    )(neighbours, energy_weights, valence, parts(single_site), parts(structure), gaunt_table, shapes,
      radial_weights[None, :], species[None, :], madelung,
      jnp.transpose(old_potential, (1, 0, 2)))

    back = lambda x: jnp.transpose(x, (1, 0, 2))
    return back(density), back(potential)


def solution(mesh):
    in_specs = (
        P("atom", "energy", None, None),
        P("energy", None, None, None),
        P("atom", None),
        P("atom"),
        P(),
        P("energy", None),
        P(),
        P(None, "energy", None, None, None),
        P(),
        P("atom", None),
        P("atom", None, "energy"),
    )
    out_specs = (P("atom", None, "energy"), P("atom", None, "energy"))
    return jax.shard_map(shards, mesh=mesh, in_specs=in_specs, out_specs=out_specs, check_vma=False)
```

profile of v0, /device:TPU:0, one launch (start us, length us, event | category | flops | bytes accessed | tf_op | source)
XLA Modules:
  0.0 25.3 jit_solution(8954109702901056186)
XLA Ops:
  0.6 21.7 %scatter.1 = (f32[49,16,256]{2,1,0:T(8,128)}, f32[49,16,256]{2,1,0:T(8,128)}) custom-call(s32[16,26]{1,0:T(8,128)} %nbr_ref.1, f32[1,2]{1,0:T(1,128)} %w_ref.1, f32[2]{0:T(128)} %valence_ref.1, f32[8,2,2,1024]{3,2,1,0:T(2,128)} %bitcast.15, f32[13,2,2,1024]{3,2,1,0:T(2,128)} %bitcast.14, f32[49,1024]{1,0:T(8,128)} %gaunt_ref.1, f32[2,49,2,512]{3,2,1,0:T(2,128)} %bitcast.13, ...), custom_call_target="tpu_custom_call" | custom-call | tf_op jit(solution)/shard_map/scatter/pallas_call | solution.py:416
  22.3 0.0 copy-start
  22.3 2.2 %copy.15 = f32[16,49,256]{2,0,1:T(8,128)} copy(f32[16,49,256]{2,0,1:T(8,128)} %bitcast.12) | data formatting | bytes 1605632
  24.5 0.0 copy-done
  24.5 0.9 %copy.16 = f32[16,49,256]{2,0,1:T(8,128)} copy(f32[16,49,256]{2,0,1:T(8,128)S(1)} %bitcast.11) | data formatting | bytes 1605632
Async XLA Ops:
  22.3 2.2 %copy-start = (f32[49,16,256]{2,1,0:T(8,128)S(1)}, f32[49,16,256]{2,1,0:T(8,128)}, u32[]{:S(2)}) copy-start(f32[49,16,256]{2,1,0:T(8,128)} %get-tuple-element.5) | copy-start | bytes 2408452
where the time goes:
time: 25.5 us; the launch traced here: 25.3 us
  Pallas kernels  21.7 us (85%)
  local copies, waits for them, and re-layouts  3.04 us (12%)
  between operations  0.65 us (3%)
    pallas_call x1, Pallas kernels, shards(): pl.pallas_call(functools.partial(core, order, dirs, ring, energies), out_...  21.7 us
    unnamed x4, local copies, waits for them, and re-layouts  3.04 us

commit v1 on v0

v1 whole, which is shorter than its diff:
```python
import functools

import jax
import jax.numpy as jnp
from jax import lax
from jax.experimental import pallas as pl
from jax.experimental.pallas import tpu as pltpu
from jax.sharding import PartitionSpec as P

PLANE = 16
LANES = 128
ROWS = 8
CHUNKS = 4

mixing = 0.3
f32 = jnp.float32
bf16 = jnp.bfloat16


def split(x):
    high = x.astype(bf16)
    return high, (x - high.astype(f32)).astype(bf16)


def dot(a, b):
    return jnp.dot(a, b, preferred_element_type=f32)


def lane_masks(rows):
    lane = lax.broadcasted_iota(jnp.int32, (rows, LANES), 1)
    return lane < 64, (lane & 32) == 0


def times_i(x, real_lane):
    return jnp.where(real_lane, -pltpu.roll(x, 96, 1), pltpu.roll(x, 32, 1))


def swap_blocks(parts):
    low, even = lane_masks(parts[0].shape[0])
    near = []
    for a, b in ((parts[0], parts[1]), (parts[2], parts[3])):
        near.append((jnp.where(even, a, pltpu.roll(b, 32, 1)), jnp.where(even, pltpu.roll(a, 96, 1), b)))
    out = [None] * 4
    for j in range(2):
        c, d = near[0][j], near[1][j]
        out[j] = jnp.where(low, c, pltpu.roll(d, 64, 1))
        out[j + 2] = jnp.where(low, pltpu.roll(c, 64, 1), d)
    return out


def to_tile(raw, out_ref):
    rows = swap_blocks([raw(m) for m in range(4)])
    for ii in range(4):
        out_ref[pl.ds(ii, ROWS, stride=4), :] = rows[ii]


def packed(x):
    high, low = split(x)
    half = LANES // 2
    even = jnp.concatenate([high[:, :half], low[:, :half]], axis=1)
    odd = jnp.concatenate([high[:, half:], low[:, half:]], axis=1)
    return even, odd


def block_diagonal(v, low_lane, real_lane):
    turned = times_i(v, real_lane)
    zero = jnp.zeros_like(v)
    return jnp.concatenate(
        [
            jnp.where(low_lane, v, zero),
            jnp.where(low_lane, turned, zero),
            jnp.where(low_lane, zero, v),
            jnp.where(low_lane, zero, turned),
        ],
        axis=0,
    )


def weights_of(v, low_lane, real_lane):
    high, low = split(block_diagonal(v, low_lane, real_lane))
    return jnp.concatenate([high, low], axis=1)


def pair_product(u, weights):
    rows = u.shape[0]
    high, low = split(u)
    o = dot(jnp.concatenate([high, low], axis=0), weights)
    return o[:rows, :LANES] + o[rows:, :LANES] + o[:rows, LANES:]


def ends_of(dirs):
    return ((0, 9), (9, 17), (17, dirs))


def plane_products(tiles, gx_ref, l_ref, start, stop, order):
    count = stop - start
    lhs = gx_ref[start:stop, :order, :].reshape(count * order, LANES)
    lhs = jnp.concatenate([lhs, lhs], axis=1)
    _, real_lane = lane_masks(order)
    for quad in range(PLANE // 4):
        columns = []
        for pair in (2 * quad, 2 * quad + 1):
            v = tiles[pair]
            high, low = split(jnp.concatenate([v, times_i(v, real_lane)], axis=0))
            columns.append(jnp.concatenate([high, high, low, low], axis=0))
        r = dot(lhs, jnp.concatenate(columns, axis=1))
        for h in range(2):
            even, odd = packed(r[:, h * LANES : (h + 1) * LANES])
            n = 4 * quad + 2 * h
            l_ref[start:stop, n] = even.reshape(count, order, LANES)
            l_ref[start:stop, n + 1] = odd.reshape(count, order, LANES)


def plane_sum(nbr_ref, gx_ref, l_ref, start, stop, dirs):
    lhs, rhs = [], []
    for a in range(PLANE):
        lhs.append(jnp.concatenate([l_ref[k, nbr_ref[a, k] & (PLANE - 1)] for k in range(start, stop)], axis=1))
    for k in range(start, stop):
        g = gx_ref[dirs - 1 - k]
        rhs += [g, g]
    return dot(jnp.concatenate(lhs, axis=0), jnp.concatenate(rhs, axis=0))


def project(tiles, total, wd_ref, table_ref, v_ref, order):
    low_lane, real_lane = lane_masks(order)
    pairs = range(PLANE // 2)
    cs = []
    for pair in pairs:
        even = total[2 * pair * order : (2 * pair + 1) * order]
        odd = total[(2 * pair + 1) * order : (2 * pair + 2) * order]
        cs.append(jnp.where(low_lane, even, odd) + pltpu.roll(jnp.where(low_lane, odd, even), 64, 1))
    qs = [pair_product(cs[pair], wd_ref[pair]) for pair in pairs]
    ws = [weights_of(q, low_lane, real_lane) for q in qs]
    ts = [tiles[pair] for pair in pairs]
    ys = [pair_product(jnp.concatenate([ts[pair], qs[pair]], axis=0), ws[pair]) for pair in pairs]
    vs = [ts[pair] + ys[pair][:order] for pair in pairs]
    ws = [weights_of(y[order:], low_lane, real_lane) for y in ys]
    for pair in pairs:
        v_ref[pl.ds(pair * order, order), :] = vs[pair] + pair_product(vs[pair], ws[pair])
    columns = []
    for block in range(order // 4):
        us = [v_ref[pl.ds(4 * block + ii, PLANE // 2, stride=order), :] for ii in range(4)]
        columns.append(jnp.concatenate(swap_blocks(us), axis=0))
    z = jnp.concatenate(columns, axis=1)
    zh, zl = split(z)
    nt = (((1,), (1,)), ((), ()))
    d = lax.dot_general(jnp.concatenate([zh, zl], axis=0), table_ref[...], nt, preferred_element_type=f32)
    rows = 2 * PLANE
    return d[:rows] + d[rows:] + pltpu.roll(d[:rows], 64, 1)


def store_scaled(projected, wr, wi, coef_ref):
    pairs = PLANE // 2
    channels = coef_ref.shape[2]
    for a2 in range(2):
        re = projected[a2 * 2 * pairs : a2 * 2 * pairs + pairs, :channels]
        im = projected[a2 * 2 * pairs + pairs : (a2 + 1) * 2 * pairs, :channels]
        coef_ref[0, pl.ds(a2, pairs, stride=2), :] = wr * re - wi * im
        coef_ref[1, pl.ds(a2, pairs, stride=2), :] = wr * im + wi * re


def density_of(kind, coef_ref, pieces_ref, old_ref, density_ref, potential_ref):
    energies, kinds = pieces_ref.shape[:2]
    channels, atoms, width = density_ref.shape
    kind = jnp.broadcast_to(kind, (atoms, width))
    for l in range(channels):
        total = None
        for e in range(energies):
            for z in range(2):
                row = jnp.broadcast_to(pieces_ref[e, 0, l, 1 - z : 2 - z, :], (atoms, width))
                for s in range(1, kinds):
                    row = jnp.where(kind == s, pieces_ref[e, s, l, 1 - z : 2 - z, :], row)
                term = coef_ref[e, z, :, l : l + 1] * row
                total = term if total is None else total + term
        density_ref[l] = total
        if l > 0:
            potential_ref[l] = (1.0 - mixing) * old_ref[l] + mixing * total


def far_rounds(ring):
    rounds = 0
    while 2**rounds < ring // 2:
        rounds += 1
    return rounds


def core(order, dirs, ring, energies,
         nbr_hbm, w_hbm, valence_hbm, own_hbm, g_hbm, gaunt_hbm, shapes_hbm, weights_hbm, species_hbm,
         madelung_hbm, previous_hbm, density_ref, potential_ref,
         nbr_ref, w_ref, valence_ref, own_ref, g_ref, gaunt_ref, lowest_ref, weights_ref, species_ref,
         madelung_ref, old_ref, pieces_ref, coef_ref, mine_ref, q_ref, halo_ref,
         gtile_ref, tile_ref, gx_ref, l_ref, wd_ref, table_ref, v_ref,
         load_sem, keep_sem, halo_send, halo_recv, piece_send, piece_recv, coef_send, coef_recv,
         q_send, q_recv, far_sem):
    atom, energy = lax.axis_index("atom"), lax.axis_index("energy")
    devices = ring * energies
    me = atom * energies + energy
    kinds, width = shapes_hbm.shape[0], pieces_ref.shape[4]
    channels = gaunt_ref.shape[0]
    ends = ends_of(dirs)

    def ahead(step):
        return {"atom": lax.rem(atom + step + ring, ring), "energy": energy}

    def peer(step):
        return {"atom": atom, "energy": lax.rem(energy + step, energies)}

    barrier = pltpu.get_barrier_semaphore()
    near = [ahead(1), ahead(-1)] + [peer(step) for step in range(1, energies)]
    for place in near:
        pl.semaphore_signal(barrier, inc=1, device_id=place, device_id_type=MESH)

    sources = [(own_hbm, own_ref), (g_hbm, g_ref), (nbr_hbm, nbr_ref), (gaunt_hbm, gaunt_ref),
               (shapes_hbm.at[:, 0], lowest_ref), (weights_hbm, weights_ref), (species_hbm, species_ref),
               (w_hbm, w_ref), (valence_hbm, valence_ref), (madelung_hbm, madelung_ref), (previous_hbm, old_ref)]
    loads = []
    for i, (src, dst) in enumerate(sources):
        loads.append(pltpu.make_async_copy(src, dst, load_sem.at[i]))
        loads[-1].start()

    loads[0].wait()
    pl.semaphore_wait(barrier, len(near))
    rounds = far_rounds(ring)

    def tell(index):
        places = [ahead(2**index), ahead(-(2**index))] if index < rounds else near[2:]
        for place in places:
            pl.semaphore_signal(far_sem.at[index], inc=1, device_id=place, device_id_type=MESH)

    def hear(index):
        pl.semaphore_wait(far_sem.at[index], 2 if index < rounds else energies - 1)

    tell(0)
    halos = []
    for side, step in ((0, 1), (1, -1)):
        copy = pltpu.make_async_remote_copy(
            src_ref=own_ref, dst_ref=halo_ref.at[side], send_sem=halo_send.at[side],
            recv_sem=halo_recv.at[side], device_id=ahead(step), device_id_type=MESH,
        )
        copy.start()
        halos.append(copy)

    def slice_of(e):
        return shapes_hbm.at[:, :, :, pl.ds(pl.multiple_of(e * width, LANES), width)]

    pieces = []
    for step in range(1, energies):
        copy = pltpu.make_async_remote_copy(
            src_ref=slice_of(lax.rem(energy + step, energies)), dst_ref=pieces_ref.at[energy],
            send_sem=piece_send.at[step], recv_sem=piece_recv.at[step], device_id=peer(step), device_id_type=MESH,
        )
        copy.start()
        pieces.append(copy)
    keep = pltpu.make_async_copy(slice_of(energy), pieces_ref.at[energy], keep_sem)
    keep.start()

    loads[1].wait()
    low_lane, real_lane = lane_masks(order)
    for t in range(dirs // 2):
        to_tile(lambda m: g_ref[2 * t + m // 2, pl.ds(m % 2, ROWS, stride=2), :], gtile_ref.at[t])
        g = gtile_ref[t]
        even, odd = packed(jnp.concatenate([g, times_i(g, real_lane)], axis=0))
        gx_ref[2 * t] = even
        gx_ref[2 * t + 1] = odd

    def products(index, ref):
        for pair in range(PLANE // 2):
            to_tile(lambda m: ref[2 * pair + m // 2, pl.ds(m % 2, ROWS, stride=2), :], tile_ref.at[index, pair])
        plane_products(tile_ref.at[index], gx_ref, l_ref, *ends[index], order)

    products(1, own_ref)
    loads[2].wait()
    own_sum = plane_sum(nbr_ref, gx_ref, l_ref, *ends[1], dirs)

    for pair in range(PLANE // 2):
        wd_ref[pair] = weights_of(tile_ref[1, pair], low_lane, real_lane)
    loads[3].wait()
    high, low = split(gaunt_ref[...])
    table_ref[...] = jnp.zeros(table_ref.shape, bf16)
    table_ref[pl.ds(0, channels), :] = high
    table_ref[pl.ds(64, channels), :] = low

    for load in loads[4:10]:
        load.wait()
    row = lax.broadcasted_iota(jnp.int32, (PLANE, PLANE), 0)
    lane = lax.broadcasted_iota(jnp.int32, (PLANE, PLANE), 1)
    kinds_row = jnp.broadcast_to(species_ref[...].astype(f32), (PLANE, PLANE))
    kind = jnp.sum(jnp.where(row == lane, kinds_row, jnp.zeros((PLANE, PLANE), f32)), axis=1, keepdims=True)
    sums = [None, None]
    base = jnp.zeros(kind.shape, f32)
    for s in range(kinds):
        total = jnp.sum(lowest_ref[s] * weights_ref[...], axis=1, keepdims=True)
        for z in range(2):
            value = jnp.broadcast_to(total[1 - z : 2 - z], kind.shape)
            sums[z] = value if s == 0 else jnp.where(kind == s, value, sums[z])
        base = jnp.where(kind == s, valence_ref[s], base)
    base = jnp.where(energy == 0, base, jnp.zeros_like(base))

    total = own_sum
    hear(0)
    tell(1)
    halos[0].wait_recv()
    products(0, halo_ref.at[0])
    total = total + plane_sum(nbr_ref, gx_ref, l_ref, *ends[0], dirs)
    hear(1)
    tell(2)
    halos[1].wait_recv()
    products(2, halo_ref.at[1])
    total = total + plane_sum(nbr_ref, gx_ref, l_ref, *ends[2], dirs)
    for index in range(2, rounds):
        hear(index)
        tell(index + 1)

    projected = project(tile_ref.at[1], total, wd_ref, table_ref, v_ref, order)
    store_scaled(projected, w_ref[0, 0], w_ref[0, 1], mine_ref)

    q = mine_ref[0, :, 0:1] * sums[0] + mine_ref[1, :, 0:1] * sums[1] - base
    row = lax.broadcasted_iota(jnp.int32, (PLANE, LANES), 0)
    lane = lax.broadcasted_iota(jnp.int32, (PLANE, LANES), 1)
    spot = lane == row + PLANE * lax.rem(atom, LANES // PLANE)
    q_ref[me] = jnp.sum(jnp.where(spot, q, jnp.zeros((PLANE, LANES), f32)), axis=0, keepdims=True)
    hear(rounds)

    def spread(step, carry):
        other = lax.rem(me + step, devices)
        pltpu.make_async_remote_copy(
            src_ref=q_ref.at[me], dst_ref=q_ref.at[me], send_sem=q_send, recv_sem=q_recv,
            device_id={"atom": other // energies, "energy": lax.rem(other, energies)}, device_id_type=MESH,
        ).start()
        return carry

    lax.fori_loop(1, devices, spread, 0)
    coefs = []
    for step in range(1, energies):
        copy = pltpu.make_async_remote_copy(
            src_ref=mine_ref, dst_ref=coef_ref.at[energy], send_sem=coef_send.at[step],
            recv_sem=coef_recv.at[step], device_id=peer(step), device_id_type=MESH,
        )
        copy.start()
        coefs.append(copy)
    coef_ref[energy] = mine_ref[...]

    keep.wait()
    loads[10].wait()
    for copy in pieces + coefs:
        copy.wait()
    density_of(kind, coef_ref, pieces_ref, old_ref, density_ref, potential_ref)
    for copy in halos:
        copy.wait_send()
    rest = q_ref.at[pl.ds(0, devices - 1)]
    pltpu.make_async_copy(rest, rest, q_send).wait()
    pltpu.make_async_copy(rest, rest, q_recv).wait()
    group = LANES // PLANE * energies
    shift = jnp.zeros((PLANE, 1), f32)
    for g in range(ring * PLANE // LANES):
        charges = jnp.sum(q_ref[pl.ds(g * group, group), 0, :], axis=0, keepdims=True)
        shift = shift + jnp.sum(madelung_ref[:, pl.ds(g * LANES, LANES)] * charges, axis=1, keepdims=True)
    potential_ref[0] = (1.0 - mixing) * old_ref[0] + mixing * (density_ref[0] + shift)


def core_scratch(order, dirs, ring, energies, channels, kinds, width):
    dma = pltpu.SemaphoreType.DMA
    return [
        pltpu.SMEM((PLANE, dirs), jnp.int32),
        pltpu.SMEM((1, 2), f32),
        pltpu.SMEM((kinds,), f32),
        pltpu.VMEM((PLANE, 2 * ROWS, LANES), f32),
        pltpu.VMEM((dirs, 2 * ROWS, LANES), f32),
        pltpu.VMEM((channels, order * order), f32),
        pltpu.VMEM((kinds, 2, width * energies), f32),
        pltpu.VMEM((1, width * energies), f32),
        pltpu.VMEM((1, PLANE), jnp.int32),
        pltpu.VMEM((PLANE, ring * PLANE), f32),
        pltpu.VMEM((channels, PLANE, width), f32),
        pltpu.VMEM((energies, kinds, channels, 2, width), f32),
        pltpu.VMEM((energies, 2, PLANE, channels), f32),
        pltpu.VMEM((2, PLANE, channels), f32),
        pltpu.VMEM((ring * energies, 1, LANES), f32),
        pltpu.VMEM((2, PLANE, 2 * ROWS, LANES), f32),
        pltpu.VMEM((dirs // 2, order, LANES), f32),
        pltpu.VMEM((3, PLANE // 2, order, LANES), f32),
        pltpu.VMEM((dirs, 2 * order, LANES), bf16),
        pltpu.VMEM((dirs, PLANE, order, LANES), bf16),
        pltpu.VMEM((PLANE // 2, LANES, 2 * LANES), bf16),
        pltpu.VMEM((LANES, order * order), bf16),
        pltpu.VMEM((PLANE // 2 * order, LANES), f32),
        dma((11,)), dma, dma((2,)), dma((2,)), dma((energies,)), dma((energies,)), dma((energies,)),
        dma((energies,)), dma, dma, pltpu.SemaphoreType.REGULAR((far_rounds(ring) + 1,)),
    ]


def emit(density_ref, potential_ref, density_out, potential_out, sems):
    channels = density_ref.shape[0]
    edges = [channels * i // CHUNKS for i in range(CHUNKS + 1)]
    copies = []
    for i in range(CHUNKS):
        part = pl.ds(edges[i], edges[i + 1] - edges[i])
        for j, (src, dst) in enumerate(((density_ref, density_out), (potential_ref, potential_out))):
            copies.append(pltpu.make_async_copy(src.at[part], dst.at[part], sems.at[2 * i + j]))
            copies[-1].start()
    for copy in copies:
        copy.wait()


VMEM = pl.BlockSpec(memory_space=pltpu.VMEM)
ANY = pl.BlockSpec(memory_space=pl.ANY)
HBM = pl.BlockSpec(memory_space=pltpu.HBM)
MESH = pl.DeviceIdType.MESH


def shards(single_site, structure, neighbours, species, valence, energy_weights, gaunt_table,
           radial_shapes, radial_weights, madelung, old_potential):
    atom_rows, energy_rows = single_site.shape[:2]
    dirs = structure.shape[1]
    order = int(round(single_site.shape[3] ** 0.5))
    channels, width = old_potential.shape[1], old_potential.shape[2]
    kinds = radial_shapes.shape[0]
    energies = lax.axis_size("energy")
    assert atom_rows == PLANE and energy_rows == 1 and order == 32 and channels <= 64

    def parts(x):
        x = x.reshape(-1, 2, order * order // LANES, LANES)
        return jnp.transpose(x, (0, 2, 1, 3)).reshape(-1, 2 * ROWS, LANES)

    shapes = jnp.transpose(radial_shapes[:, 0], (0, 2, 1, 3))
    ring = lax.axis_size("atom")
    whole = [jax.ShapeDtypeStruct((channels, atom_rows, width), f32)] * 2
    operands = (neighbours, energy_weights, valence, parts(single_site), parts(structure), gaunt_table, shapes,
                radial_weights[None, :], species[None, :], madelung, jnp.transpose(old_potential, (1, 0, 2)))
    density, potential = pl.pallas_call(
        functools.partial(core, order, dirs, ring, energies),
        out_shape=whole,
        in_specs=[HBM] * 11,
        out_specs=[VMEM] * 2,
        scratch_shapes=core_scratch(order, dirs, ring, energies, channels, kinds, width),
        compiler_params=pltpu.CompilerParams(
            collective_id=0, has_side_effects=True, vmem_limit_bytes=32 * 1024 * 1024
        ),
        name="scatter",
    )(*(pltpu.with_memory_space_constraint(x, pltpu.HBM) for x in operands))
    density, potential = pl.pallas_call(
        emit,
        out_shape=whole,
        in_specs=[ANY] * 2,
        out_specs=[ANY] * 2,
        scratch_shapes=[pltpu.SemaphoreType.DMA((2 * CHUNKS,))],
        compiler_params=pltpu.CompilerParams(vmem_limit_bytes=1024 * 1024),
        name="emit",
    )(density, potential)

    back = lambda x: jnp.transpose(x, (1, 0, 2))
    return back(density), back(potential)


def solution(mesh):
    in_specs = (
        P("atom", "energy", None, None),
        P("energy", None, None, None),
        P("atom", None),
        P("atom"),
        P(),
        P("energy", None),
        P(),
        P(None, "energy", None, None, None),
        P(),
        P("atom", None),
        P("atom", None, "energy"),
    )
    out_specs = (P("atom", None, "energy"), P("atom", None, "energy"))
    return jax.shard_map(shards, mesh=mesh, in_specs=in_specs, out_specs=out_specs, check_vma=False)
```

time: 25.5 us -> 20.9 us (0.82)
  local copies, waits for them, and re-layouts: 3.04 us -> 0 us
  Pallas kernels: 21.7 us -> 20.1 us
    unnamed x4 -> x0, local copies, waits for them, and re-layouts: 3.04 us -> none
    pallas_call x1, Pallas kernels: 21.7 us -> 18.9 us  [shards(): pl.pallas_call(functools.partial(core, order, dirs, ring, energies), out_...]
    pallas_call x0 -> x1, Pallas kernels: none -> 1.21 us  [shards(): pl.pallas_call(emit, out_shape=whole, in_specs=[ANY] * 2, out_specs=[ANY]...]
where the time goes in v1:
time: 20.9 us; the launch traced here: 20.7 us
  Pallas kernels  20.1 us (96%)
  between operations  0.64 us (3%)
    pallas_call x1, Pallas kernels, shards(): pl.pallas_call(functools.partial(core, order, dirs, ring, energies), out_...  18.9 us
    pallas_call x1, Pallas kernels, shards(): pl.pallas_call(emit, out_shape=whole, in_specs=[ANY] * 2, out_specs=[ANY]...  1.21 us

profile of v1, /device:TPU:0, one launch (start us, length us, event | category | flops | bytes accessed | tf_op | source)
XLA Modules:
  0.0 20.7 jit_solution(6161807704842737493)
XLA Ops:
  0.6 18.9 %scatter.1 = (f32[49,16,256]{2,1,0:T(8,128)S(1)}, f32[49,16,256]{2,1,0:T(8,128)S(1)}) custom-call(s32[16,26]{1,0:T(8,128)} %nbr_hbm.1, f32[1,2]{1,0:T(1,128)} %w_hbm.1, f32[2]{0:T(128)} %valence_hbm.1, f32[16,16,128]{2,1,0:T(8,128)} %bitcast.21, f32[26,16,128]{2,1,0:T(8,128)} %bitcast.20, f32[49,1024]{1,0:T(8,128)} %gaunt_hbm.1, f32[2,49,2,512]{3,2,1,0:T(2,128)} %bitcast.19, ...), custom_call_target="tpu_custom_call" | custom-call | tf_op jit(solution)/shard_map/scatter/pallas_call | solution.py:430
  19.5 1.2 %emit.1 = (f32[49,16,256]{2,1,0:T(8,128)}, f32[49,16,256]{2,1,0:T(8,128)}) custom-call(f32[49,16,256]{2,1,0:T(8,128)S(1)} %get-tuple-element.6.density_ref, f32[49,16,256]{2,1,0:T(8,128)S(1)} %get-tuple-element.7.potential_ref), custom_call_target="tpu_custom_call" | custom-call | tf_op jit(solution)/shard_map/emit/pallas_call | solution.py:441

commit v2 on v1

--- a/solution.py
+++ b/solution.py
@@ -11,6 +11,7 @@
 LANES = 128
 ROWS = 8
 CHUNKS = 4
+PARTS = 1
 
 mixing = 0.3
 f32 = jnp.float32
@@ -107,36 +108,39 @@
         for h in range(2):
             even, odd = packed(r[:, h * LANES : (h + 1) * LANES])
             n = 4 * quad + 2 * h
-            l_ref[start:stop, n] = even.reshape(count, order, LANES)
-            l_ref[start:stop, n + 1] = odd.reshape(count, order, LANES)
-
-
-def plane_sum(nbr_ref, gx_ref, l_ref, start, stop, dirs):
+            l_ref[:count, n] = even.reshape(count, order, LANES)
+            l_ref[:count, n + 1] = odd.reshape(count, order, LANES)
+
+
+def plane_sum(nbr_ref, gx_ref, l_ref, start, stop, dirs, atoms):
     lhs, rhs = [], []
-    for a in range(PLANE):
-        lhs.append(jnp.concatenate([l_ref[k, nbr_ref[a, k] & (PLANE - 1)] for k in range(start, stop)], axis=1))
+    for a in atoms:
+        lhs.append(jnp.concatenate([l_ref[k - start, nbr_ref[a, k] & (PLANE - 1)] for k in range(start, stop)], axis=1))
     for k in range(start, stop):
         g = gx_ref[dirs - 1 - k]
         rhs += [g, g]
     return dot(jnp.concatenate(lhs, axis=0), jnp.concatenate(rhs, axis=0))
 
 
-def project(tiles, total, wd_ref, table_ref, v_ref, order):
+def series(tiles, total, wd_ref, v_ref, atoms, order):
     low_lane, real_lane = lane_masks(order)
-    pairs = range(PLANE // 2)
-    cs = []
-    for pair in pairs:
-        even = total[2 * pair * order : (2 * pair + 1) * order]
-        odd = total[(2 * pair + 1) * order : (2 * pair + 2) * order]
-        cs.append(jnp.where(low_lane, even, odd) + pltpu.roll(jnp.where(low_lane, odd, even), 64, 1))
-    qs = [pair_product(cs[pair], wd_ref[pair]) for pair in pairs]
-    ws = [weights_of(q, low_lane, real_lane) for q in qs]
-    ts = [tiles[pair] for pair in pairs]
-    ys = [pair_product(jnp.concatenate([ts[pair], qs[pair]], axis=0), ws[pair]) for pair in pairs]
-    vs = [ts[pair] + ys[pair][:order] for pair in pairs]
-    ws = [weights_of(y[order:], low_lane, real_lane) for y in ys]
+    pairs = range(atoms[0] // 2, atoms[-1] // 2 + 1)
+    cs = {}
+    for i, pair in enumerate(pairs):
+        even = total[2 * i * order : (2 * i + 1) * order]
+        odd = total[(2 * i + 1) * order : (2 * i + 2) * order]
+        cs[pair] = jnp.where(low_lane, even, odd) + pltpu.roll(jnp.where(low_lane, odd, even), 64, 1)
+    ts = {pair: tiles[pair] for pair in pairs}
+    qs = {pair: pair_product(cs[pair], wd_ref[pair]) for pair in pairs}
+    ws = {pair: weights_of(qs[pair], low_lane, real_lane) for pair in pairs}
+    ys = {pair: pair_product(jnp.concatenate([ts[pair], qs[pair]], axis=0), ws[pair]) for pair in pairs}
+    vs = {pair: ts[pair] + ys[pair][:order] for pair in pairs}
+    ws = {pair: weights_of(ys[pair][order:], low_lane, real_lane) for pair in pairs}
     for pair in pairs:
         v_ref[pl.ds(pair * order, order), :] = vs[pair] + pair_product(vs[pair], ws[pair])
+
+
+def project(table_ref, v_ref, order):
     columns = []
     for block in range(order // 4):
         us = [v_ref[pl.ds(4 * block + ii, PLANE // 2, stride=order), :] for ii in range(4)]
@@ -189,7 +193,7 @@
          madelung_hbm, previous_hbm, density_ref, potential_ref,
          nbr_ref, w_ref, valence_ref, own_ref, g_ref, gaunt_ref, lowest_ref, weights_ref, species_ref,
          madelung_ref, old_ref, pieces_ref, coef_ref, mine_ref, q_ref, halo_ref,
-         gtile_ref, tile_ref, gx_ref, l_ref, wd_ref, table_ref, v_ref,
+         gtile_ref, tile_ref, gx_ref, l0_ref, l1_ref, l2_ref, c_ref, wd_ref, table_ref, v_ref,
          load_sem, keep_sem, halo_send, halo_recv, piece_send, piece_recv, coef_send, coef_recv,
          q_send, q_recv, far_sem):
     atom, energy = lax.axis_index("atom"), lax.axis_index("energy")
@@ -198,6 +202,7 @@
     kinds, width = shapes_hbm.shape[0], pieces_ref.shape[4]
     channels = gaunt_ref.shape[0]
     ends = ends_of(dirs)
+    l_refs = (l0_ref, l1_ref, l2_ref)
 
     def ahead(step):
         return {"atom": lax.rem(atom + step + ring, ring), "energy": energy}
@@ -266,11 +271,11 @@
     def products(index, ref):
         for pair in range(PLANE // 2):
             to_tile(lambda m: ref[2 * pair + m // 2, pl.ds(m % 2, ROWS, stride=2), :], tile_ref.at[index, pair])
-        plane_products(tile_ref.at[index], gx_ref, l_ref, *ends[index], order)
+        plane_products(tile_ref.at[index], gx_ref, l_refs[index], *ends[index], order)
 
     products(1, own_ref)
     loads[2].wait()
-    own_sum = plane_sum(nbr_ref, gx_ref, l_ref, *ends[1], dirs)
+    c_ref[...] = plane_sum(nbr_ref, gx_ref, l_refs[1], *ends[1], dirs, range(PLANE))
 
     for pair in range(PLANE // 2):
         wd_ref[pair] = weights_of(tile_ref[1, pair], low_lane, real_lane)
@@ -296,22 +301,25 @@
         base = jnp.where(kind == s, valence_ref[s], base)
     base = jnp.where(energy == 0, base, jnp.zeros_like(base))
 
-    total = own_sum
     hear(0)
     tell(1)
     halos[0].wait_recv()
     products(0, halo_ref.at[0])
-    total = total + plane_sum(nbr_ref, gx_ref, l_ref, *ends[0], dirs)
+    c_ref[...] += plane_sum(nbr_ref, gx_ref, l_refs[0], *ends[0], dirs, range(PLANE))
     hear(1)
     tell(2)
     halos[1].wait_recv()
     products(2, halo_ref.at[1])
-    total = total + plane_sum(nbr_ref, gx_ref, l_ref, *ends[2], dirs)
     for index in range(2, rounds):
         hear(index)
         tell(index + 1)
 
-    projected = project(tile_ref.at[1], total, wd_ref, table_ref, v_ref, order)
+    for part in range(PARTS):
+        atoms = range(part * PLANE // PARTS, (part + 1) * PLANE // PARTS)
+        rows = pl.ds(atoms[0] * order, len(atoms) * order)
+        total = c_ref[rows, :] + plane_sum(nbr_ref, gx_ref, l_refs[2], *ends[2], dirs, atoms)
+        series(tile_ref.at[1], total, wd_ref, v_ref, atoms, order)
+    projected = project(table_ref, v_ref, order)
     store_scaled(projected, w_ref[0, 0], w_ref[0, 1], mine_ref)
 
     q = mine_ref[0, :, 0:1] * sums[0] + mine_ref[1, :, 0:1] * sums[1] - base
@@ -321,15 +329,22 @@
     q_ref[me] = jnp.sum(jnp.where(spot, q, jnp.zeros((PLANE, LANES), f32)), axis=0, keepdims=True)
     hear(rounds)
 
-    def spread(step, carry):
-        other = lax.rem(me + step, devices)
-        pltpu.make_async_remote_copy(
-            src_ref=q_ref.at[me], dst_ref=q_ref.at[me], send_sem=q_send, recv_sem=q_recv,
-            device_id={"atom": other // energies, "energy": lax.rem(other, energies)}, device_id_type=MESH,
-        ).start()
-        return carry
-
-    lax.fori_loop(1, devices, spread, 0)
+    def spread(ahead_by):
+        place = lax.rem(atom + ahead_by, ring)
+        for step in range(energies):
+            if isinstance(ahead_by, int) and ahead_by == 0 and step == 0:
+                continue
+            pltpu.make_async_remote_copy(
+                src_ref=q_ref.at[me], dst_ref=q_ref.at[me], send_sem=q_send, recv_sem=q_recv,
+                device_id={"atom": place, "energy": lax.rem(energy + step, energies)}, device_id_type=MESH,
+            ).start()
+
+    if ring <= 2 * PLANE:
+        for ahead_by in sorted(range(1, ring), key=lambda d: -min(d, ring - d)):
+            spread(ahead_by)
+    else:
+        lax.fori_loop(1, ring, lambda d, carry: (spread(d), carry)[1], 0)
+    spread(0)
     coefs = []
     for step in range(1, energies):
         copy = pltpu.make_async_remote_copy(
@@ -380,7 +395,8 @@
         pltpu.VMEM((dirs // 2, order, LANES), f32),
         pltpu.VMEM((3, PLANE // 2, order, LANES), f32),
         pltpu.VMEM((dirs, 2 * order, LANES), bf16),
-        pltpu.VMEM((dirs, PLANE, order, LANES), bf16),
+        *(pltpu.VMEM((stop - start, PLANE, order, LANES), bf16) for start, stop in ends_of(dirs)),
+        pltpu.VMEM((PLANE * order, LANES), f32),
         pltpu.VMEM((PLANE // 2, LANES, 2 * LANES), bf16),
         pltpu.VMEM((LANES, order * order), bf16),
         pltpu.VMEM((PLANE // 2 * order, LANES), f32),

time: 20.9 us -> 21.4 us (1.024)
  Pallas kernels: 20.1 us -> 20.6 us
    pallas_call x1, Pallas kernels: 18.9 us -> 19.4 us  [shards(): pl.pallas_call(functools.partial(core, order, dirs, ring, energies), out_...]
where the time goes in v2:
time: 21.4 us; the launch traced here: 21.3 us
  Pallas kernels  20.6 us (96%)
  between operations  0.64 us (3%)
    pallas_call x1, Pallas kernels, shards(): pl.pallas_call(functools.partial(core, order, dirs, ring, energies), out_...  19.4 us
    pallas_call x1, Pallas kernels, shards(): pl.pallas_call(emit, out_shape=whole, in_specs=[ANY] * 2, out_specs=[ANY]...  1.21 us

profile of v2, /device:TPU:0, one launch (start us, length us, event | category | flops | bytes accessed | tf_op | source)
XLA Modules:
  0.0 21.3 jit_solution(5103435376497704303)
XLA Ops:
  0.6 19.4 %scatter.1 = (f32[49,16,256]{2,1,0:T(8,128)S(1)}, f32[49,16,256]{2,1,0:T(8,128)S(1)}) custom-call(s32[16,26]{1,0:T(8,128)} %nbr_hbm.1, f32[1,2]{1,0:T(1,128)} %w_hbm.1, f32[2]{0:T(128)} %valence_hbm.1, f32[16,16,128]{2,1,0:T(8,128)} %bitcast.21, f32[26,16,128]{2,1,0:T(8,128)} %bitcast.20, f32[49,1024]{1,0:T(8,128)} %gaunt_hbm.1, f32[2,49,2,512]{3,2,1,0:T(2,128)} %bitcast.19, ...), custom_call_target="tpu_custom_call" | custom-call | tf_op jit(solution)/shard_map/scatter/pallas_call | solution.py:446
  20.0 1.2 %emit.1 = (f32[49,16,256]{2,1,0:T(8,128)}, f32[49,16,256]{2,1,0:T(8,128)}) custom-call(f32[49,16,256]{2,1,0:T(8,128)S(1)} %get-tuple-element.6.density_ref, f32[49,16,256]{2,1,0:T(8,128)S(1)} %get-tuple-element.7.potential_ref), custom_call_target="tpu_custom_call" | custom-call | tf_op jit(solution)/shard_map/emit/pallas_call | solution.py:457
